TPU v7x, 32 devices: a whole 2x2x4 slice. The times are simulated.
32 devices in a mesh: shard: 4 (over y, x), ctx: 2 (over core), tp: 4 (over z).
Axes of the slice: x: 2, y: 2, z: 4, core: 2. Of those that a mesh axis runs over, the one named last changes fastest.
Arguments:
- tokens: bfloat16 [8192, 1024], P(('shard', 'ctx')), may hold values from -6 to 6
- segment_ids: int32 [4, 2048], P('shard'), may hold values from 0 to 3, never falling along the last dimension, each value on 1 to 1024 neighbouring positions
- cotangent: bfloat16 [8192, 1024], P(('shard', 'ctx')), may hold values from -6 to 6
- mixer_gain: float32 [1024], replicated, may hold values from 0.5 to 1.5
- query_weight: bfloat16 [1024, 1024], P('shard', 'tp'), may hold values from -0.1875 to 0.1875
- key_weight: bfloat16 [1024, 1024], P('shard', 'tp'), may hold values from -0.1875 to 0.1875
- value_weight: bfloat16 [1024, 2048], P('shard', 'tp'), may hold values from -0.1875 to 0.1875
- gate_weight: bfloat16 [1024, 2048], P('shard', 'tp'), may hold values from -0.1875 to 0.1875
- decay_weight: bfloat16 [1024, 8], P('shard', 'tp'), may hold values from -0.1875 to 0.1875
- beta_weight: bfloat16 [1024, 8], P('shard', 'tp'), may hold values from -0.1875 to 0.1875
- query_conv: float32 [4, 1024], P(None, 'tp'), may hold values from -2 to 2
- key_conv: float32 [4, 1024], P(None, 'tp'), may hold values from -2 to 2
- value_conv: float32 [4, 2048], P(None, 'tp'), may hold values from -2 to 2
- decay_log: float32 [8], P('tp'), may hold values from -7.6 to -2.3
- decay_bias: float32 [8], P('tp'), may hold values from -3 to 3
- out_gain: float32 [256], replicated, may hold values from 0.5 to 1.5
- output_weight: bfloat16 [2048, 1024], P('tp', 'shard'), may hold values from -0.1875 to 0.1875
- hidden_gain: float32 [1024], replicated, may hold values from 0.5 to 1.5
- hidden_gate: bfloat16 [1024, 2816], P('shard', 'tp'), may hold values from -0.1875 to 0.1875
- hidden_up: bfloat16 [1024, 2816], P('shard', 'tp'), may hold values from -0.1875 to 0.1875
- hidden_down: bfloat16 [2816, 1024], P('tp', 'shard'), may hold values from -0.15625 to 0.15625
Outputs:
- block_out: bfloat16 [8192, 1024], P(('shard', 'ctx'))
- input_grad: float32 [8192, 1024], P(('shard', 'ctx'))
- mixer_gain_grad: float32 [1024], replicated
- query_weight_grad: float32 [1024, 1024], P('shard', 'tp')
- key_weight_grad: float32 [1024, 1024], P('shard', 'tp')
- value_weight_grad: float32 [1024, 2048], P('shard', 'tp')
- gate_weight_grad: float32 [1024, 2048], P('shard', 'tp')
- decay_weight_grad: float32 [1024, 8], P('shard', 'tp')
- beta_weight_grad: float32 [1024, 8], P('shard', 'tp')
- query_conv_grad: float32 [4, 1024], P(None, 'tp')
- key_conv_grad: float32 [4, 1024], P(None, 'tp')
- value_conv_grad: float32 [4, 2048], P(None, 'tp')
- decay_log_grad: float32 [8], P('tp')
- decay_bias_grad: float32 [8], P('tp')
- out_gain_grad: float32 [256], replicated
- output_weight_grad: float32 [2048, 1024], P('tp', 'shard')
- hidden_gain_grad: float32 [1024], replicated
- hidden_gate_grad: float32 [1024, 2816], P('shard', 'tp')
- hidden_up_grad: float32 [1024, 2816], P('shard', 'tp')
- hidden_down_grad: float32 [2816, 1024], P('tp', 'shard')
Inputs may be any that keep to these rules, and one draw needn't show every extreme that they name: `segment_ids`: within each packed row the document numbers never fall; each document has 1 to 1024 tokens and one has exactly 1024.
All inputs are finite; a program needn't handle non-finite values.
Results may differ from a plain program's by a relative error of at most 0.015.
The roundings to bfloat16 on the way count: a program that leaves them out, or rounds other values in their place, can miss the bound.
Values may be sent and summed in bfloat16 or wider, within the bound.
A program may use at most 256 MiB of HBM per device.

v0:
```python
import jax
import jax.numpy as jnp
from jax import lax
from jax.sharding import PartitionSpec as P

GROUP = 128
HIGH = lax.Precision.HIGHEST
PRECISE = lax.Precision.HIGH


def from_behind(block, axis, distance):
    devices = range(lax.axis_size(axis))
    route = [(i - distance, i) for i in devices if i - distance in devices]
    return lax.ppermute(block, axis, route)


def dot_plain(left, right):
    return jnp.dot(left, right, preferred_element_type=jnp.float32)


def dot_first(left, right):
    return lax.dot_general(
        left, right, (((0,), (0,)), ((), ())), preferred_element_type=jnp.float32
    )


def dot_second(left, right):
    return lax.dot_general(
        left, right, (((1,), (1,)), ((), ())), preferred_element_type=jnp.float32
    )


def rms_norm(values, gain):
    return values * lax.rsqrt(jnp.mean(values * values, axis=-1, keepdims=True) + 1e-06) * gain


def unit_rows(values):
    return values * lax.rsqrt(jnp.sum(values * values, axis=-1, keepdims=True) + 1e-06)


def convolve(projected, rim_rows, weights, seg_ext):
    tok_rows = projected.shape[0]
    taps = weights.shape[0]
    extended = jnp.concatenate([rim_rows, projected], axis=0)
    seg_now = seg_ext[taps - 1 :]
    summed = jnp.zeros_like(projected)
    for offset in range(taps):
        begin = taps - 1 - offset
        linked = (seg_ext[begin : begin + tok_rows] == seg_now).astype(jnp.float32)
        summed = summed + weights[offset] * extended[begin : begin + tok_rows] * linked[:, None]
    return jax.nn.silu(summed)


def dot_high(equation, left, right):
    return jnp.einsum(equation, left, right, precision=PRECISE)


@jax.custom_vjp
def unit_lower_inverse(strict_part):
    size = strict_part.shape[-1]
    order = jnp.arange(size)
    above, across = (order[:, None], order[None, :])
    inverse = jnp.broadcast_to(jnp.eye(size, dtype=jnp.float32), strict_part.shape)
    width = 1
    while width < size:
        paired = (above // (2 * width) == across // (2 * width)) & (
            above // width != across // width
        )
        coupling = jnp.where(paired, strict_part, 0.0)
        if width > 1:
            coupling = dot_high("...ij,...jk->...ik", coupling, inverse)
            coupling = dot_high("...ij,...jk->...ik", inverse, coupling)
        inverse = inverse - coupling
        width *= 2
    return inverse


def inverse_keep(strict_part):
    inverse = unit_lower_inverse(strict_part)
    return (inverse, inverse)


def inverse_pull(inverse, grad):
    inner = dot_high("...ij,...kj->...ik", grad, inverse)
    return (-dot_high("...ji,...jk->...ik", inverse, inner),)


unit_lower_inverse.defvjp(inverse_keep, inverse_pull)


def prepare(floats, seg_ext, key_dim, block_len):
    (
        q_proj,
        k_proj,
        v_proj,
        q_rim,
        k_rim,
        v_rim,
        a_proj,
        b_proj,
        q_conv,
        k_conv,
        v_conv,
        decay_log,
        decay_bias,
    ) = floats
    tok_rows = q_proj.shape[0]
    num_heads = a_proj.shape[1]
    taps = q_conv.shape[0]
    blocks = tok_rows // block_len

    def split(array):
        shaped = array.reshape(blocks, block_len, num_heads, -1)
        return jnp.transpose(shaped, (2, 0, 1, 3))

    query = unit_rows(split(convolve(q_proj, q_rim, q_conv, seg_ext))) * key_dim ** (-0.5)
    keys = unit_rows(split(convolve(k_proj, k_rim, k_conv, seg_ext)))
    values = split(convolve(v_proj, v_rim, v_conv, seg_ext))
    val_dim = values.shape[3]
    beta = jax.nn.sigmoid(b_proj).T.reshape(num_heads, blocks, block_len)
    log_gate = (-jnp.exp(decay_log) * jax.nn.softplus(a_proj + decay_bias)).T
    log_gate = log_gate.reshape(num_heads, blocks, block_len)
    seg_now = seg_ext[taps - 1 :].reshape(blocks, block_len)
    seg_before = seg_ext[taps - 2 : taps - 2 + tok_rows : block_len]
    order = jnp.arange(block_len)
    until = (order[:, None] <= order[None, :]).astype(jnp.float32)
    cumul = jnp.einsum("hcs,st->hct", log_gate, until, precision=HIGH)
    causal = (order[:, None] >= order[None, :]) & (seg_now[:, :, None] == seg_now[:, None, :])
    strict = causal & (order[:, None] > order[None, :])
    spacing = cumul[..., :, None] - cumul[..., None, :]
    within = jnp.where(causal, jnp.exp(jnp.where(causal, spacing, 0.0)), 0.0)
    from_start = jnp.where(seg_now == seg_before[:, None], jnp.exp(cumul), 0.0)
    to_end = within[..., -1, :]
    key_dots = dot_high("hctd,hcsd->hcts", keys, keys)
    inverse = unit_lower_inverse(jnp.where(strict, beta[..., None] * within * key_dots, 0.0))
    scores = dot_high("hctd,hcsd->hcts", query, keys) * within
    sources = jnp.concatenate(
        [(beta * from_start)[..., None] * keys, beta[..., None] * values], axis=-1
    )
    solved = dot_high("hcts,hcsx->hctx", inverse, sources)
    reached = dot_high("hcts,hcsx->hctx", scores, solved)
    moved = dot_high("hctx,hctd->hcxd", solved, keys * to_end[..., None])
    eye = jnp.eye(key_dim, dtype=jnp.float32)
    step_map = from_start[..., -1][..., None, None] * eye - moved[:, :, :key_dim]
    step_base = jnp.concatenate(
        [jnp.zeros((num_heads, blocks, key_dim, key_dim), jnp.float32), moved[:, :, key_dim:]],
        axis=2,
    )
    state = jnp.concatenate(
        [
            jnp.broadcast_to(eye, (num_heads, key_dim, key_dim)),
            jnp.zeros((num_heads, val_dim, key_dim), jnp.float32),
        ],
        axis=1,
    )
    states = []
    for block in range(blocks):
        states.append(state)
        state = dot_high("hxd,hde->hxe", state, step_map[:, block]) + step_base[:, block]
    entry = jnp.stack(states, axis=1)
    reading = from_start[..., None] * query - reached[..., :key_dim]
    outputs = dot_high("hctd,hcxd->hctx", reading, entry)
    mapped = outputs[..., :key_dim].reshape(num_heads, tok_rows, key_dim)
    base = (outputs[..., key_dim:] + reached[..., key_dim:]).reshape(num_heads, tok_rows, val_dim)
    return (mapped, base, state[:, :key_dim], state[:, key_dim:])


def gated_out(core, gate_proj, gain):
    num_heads, tok_rows, val_dim = core.shape
    gating = jax.nn.silu(gate_proj.reshape(tok_rows, num_heads, val_dim))
    normed = rms_norm(core, gain)
    return (jnp.transpose(normed, (1, 0, 2)) * gating).reshape(tok_rows, -1)


def swish_product(gate_pre, up_pre):
    return jax.nn.silu(gate_pre) * up_pre


def add_tail(grad_rows, incoming):
    width = incoming.shape[0]
    return jnp.concatenate([grad_rows[:-width], grad_rows[-width:] + incoming], axis=0)


def body(
    tokens,
    segment_ids,
    cotangent,
    mixer_gain,
    query_weight,
    key_weight,
    value_weight,
    gate_weight,
    decay_weight,
    beta_weight,
    query_conv,
    key_conv,
    value_conv,
    decay_log,
    decay_bias,
    out_gain,
    output_weight,
    hidden_gain,
    hidden_gate,
    hidden_up,
    hidden_down,
):
    tok_rows = tokens.shape[0]
    num_heads = decay_log.shape[0]
    key_dim = query_weight.shape[1] // num_heads
    taps = query_conv.shape[0]
    range_count = lax.axis_size("ctx")
    begin_row = lax.axis_index("ctx") * tok_rows
    seg_pad = jnp.concatenate([jnp.full((taps - 1,), -1, jnp.int32), segment_ids[0]])
    seg_ext = lax.dynamic_slice_in_dim(seg_pad, begin_row, tok_rows + taps - 1)
    low = jnp.bfloat16
    heads_wide = num_heads * key_dim
    values_wide = value_weight.shape[1]
    mixer_wide = 2 * heads_wide + 2 * values_wide
    narrow_pad = jnp.zeros((query_weight.shape[0], -2 * num_heads % 128), low)
    mixer_full = lax.all_gather(
        jnp.concatenate(
            [
                query_weight,
                key_weight,
                value_weight,
                gate_weight,
                decay_weight,
                beta_weight,
                narrow_pad,
            ],
            axis=1,
        ),
        "shard",
        axis=0,
        tiled=True,
    )
    units = hidden_gate.shape[1]
    output_full = lax.all_gather(output_weight.T, "shard", axis=0, tiled=True)
    inner_full = lax.all_gather(
        jnp.concatenate([hidden_gate, hidden_up], axis=1), "shard", axis=0, tiled=True
    )
    down_full = lax.all_gather(hidden_down.T, "shard", axis=0, tiled=True)
    part_rows = tok_rows // lax.axis_size("tp")
    part_at = lax.axis_index("tp") * part_rows

    def own_rows(array):
        return lax.dynamic_slice_in_dim(array, part_at, part_rows)

    def sum_rows(array):
        summed = lax.psum_scatter(array.astype(low), "tp", scatter_dimension=0, tiled=True)
        return summed.astype(jnp.float32)

    def all_rows(array):
        return lax.all_gather(array, "tp", axis=0, tiled=True)

    normed_low = rms_norm(tokens.astype(jnp.float32), mixer_gain).astype(low)
    x_own = own_rows(tokens).astype(jnp.float32)
    _, norm_pull = jax.vjp(rms_norm, x_own, mixer_gain)
    projected = dot_plain(normed_low, mixer_full)
    q_proj = projected[:, :heads_wide]
    k_proj = projected[:, heads_wide : 2 * heads_wide]
    v_proj = projected[:, 2 * heads_wide : 2 * heads_wide + values_wide]
    z_proj = projected[:, 2 * heads_wide + values_wide : mixer_wide]
    a_proj = projected[:, mixer_wide : mixer_wide + num_heads]
    b_proj = projected[:, mixer_wide + num_heads : mixer_wide + 2 * num_heads]
    rim = from_behind(projected[tok_rows - taps + 1 :, : 2 * heads_wide + values_wide], "ctx", 1)
    q_rim = rim[:, :heads_wide]
    k_rim = rim[:, heads_wide : 2 * heads_wide]
    v_rim = rim[:, 2 * heads_wide :]

    def local_mixer(floats):
        return prepare(floats, seg_ext, key_dim, GROUP)

    (mapped_query, base_query, state_map, state_base), prep_pull = jax.vjp(
        local_mixer,
        (
            q_proj,
            k_proj,
            v_proj,
            q_rim,
            k_rim,
            v_rim,
            a_proj,
            b_proj,
            query_conv,
            key_conv,
            value_conv,
            decay_log,
            decay_bias,
        ),
    )
    state_in = jnp.zeros_like(state_base)
    for _ in range(range_count - 1):
        ends = dot_high("hvd,hde->hve", state_in, state_map) + state_base
        state_in = from_behind(ends, "ctx", 1)
    core = base_query + dot_high("hrd,hvd->hrv", mapped_query, state_in)
    mixed, post_pull = jax.vjp(gated_out, core, z_proj, out_gain)
    mixed_low = mixed.astype(low)
    middle = x_own + sum_rows(dot_second(mixed_low, output_full))
    normed2, norm2_pull = jax.vjp(rms_norm, middle, hidden_gain)
    normed2_low = all_rows(normed2.astype(low))
    inner = dot_plain(normed2_low, inner_full)
    act, act_pull = jax.vjp(swish_product, inner[:, :units], inner[:, units:])
    act_low = act.astype(low)
    grad_act = dot_plain(cotangent, down_full)
    grad_gate, grad_up = act_pull(grad_act)
    inner_low = jnp.concatenate([grad_gate.astype(low), grad_up.astype(low)], axis=1)
    grad_normed2 = sum_rows(dot_second(inner_low, inner_full))
    ffn = sum_rows(dot_second(act_low, down_full))
    block_out = all_rows((middle + ffn).astype(low))
    grad_down = dot_first(cotangent, act_low)
    grad_inner = dot_first(normed2_low, inner_low)
    grad_mid_norm, grad_hidden_gain = norm2_pull(grad_normed2)
    grad_middle = own_rows(cotangent).astype(jnp.float32) + grad_mid_norm
    attn_low = all_rows(grad_middle.astype(low))
    grad_output = dot_first(attn_low, mixed_low)
    grad_mixed = dot_plain(attn_low, output_full)
    grad_core, grad_z, grad_out_gain = post_pull(grad_mixed)
    direct = dot_high("hrv,hrd->hvd", grad_core, mapped_query)
    grad_end = jnp.zeros_like(direct)
    for _ in range(range_count - 1):
        totals = dot_high("hve,hde->hvd", grad_end, state_map) + direct
        grad_end = from_behind(totals.astype(low), "ctx", -1).astype(totals.dtype)
    grad_mapped = dot_high("hrv,hvd->hrd", grad_core, state_in)
    grad_map = dot_high("hvd,hve->hde", state_in, grad_end)
    (float_grads,) = prep_pull((grad_mapped, grad_core, grad_map, grad_end))
    (
        grad_q,
        grad_k,
        grad_v,
        grad_q_rim,
        grad_k_rim,
        grad_v_rim,
        grad_a,
        grad_b,
        grad_q_conv,
        grad_k_conv,
        grad_v_conv,
        grad_decay_log,
        grad_decay_bias,
    ) = float_grads
    back_rim = from_behind(jnp.concatenate([grad_q_rim, grad_k_rim, grad_v_rim], axis=1), "ctx", -1)
    conv_grad = add_tail(jnp.concatenate([grad_q, grad_k, grad_v], axis=1), back_rim)
    mixer_low = jnp.concatenate(
        [
            conv_grad.astype(low),
            grad_z.astype(low),
            grad_a.astype(low),
            grad_b.astype(low),
            jnp.zeros((tok_rows, narrow_pad.shape[1]), low),
        ],
        axis=1,
    )
    grad_normed = sum_rows(dot_second(mixer_low, mixer_full))
    grad_mixer = dot_first(normed_low, mixer_low)
    grad_x_norm, grad_mixer_gain = norm_pull(grad_normed)
    input_grad = all_rows((grad_middle + grad_x_norm).astype(low)).astype(jnp.float32)

    def sum_weight(array):
        part = lax.psum_scatter(array.astype(low), "shard", scatter_dimension=0, tiled=True)
        return lax.psum(part, "ctx").astype(jnp.float32)

    sum_inner = sum_weight(jnp.concatenate([grad_inner, grad_down, grad_output], axis=1))
    sum_mixer = sum_weight(grad_mixer)
    sum_mixer_gain, sum_hidden_gain, sum_out_gain = lax.psum(
        (grad_mixer_gain, grad_hidden_gain, grad_out_gain), ("shard", "ctx", "tp")
    )
    sum_q_conv, sum_k_conv, sum_v_conv, sum_decay_log, sum_decay_bias = lax.psum(
        (grad_q_conv, grad_k_conv, grad_v_conv, grad_decay_log, grad_decay_bias), ("shard", "ctx")
    )
    return (
        block_out,
        input_grad,
        sum_mixer_gain,
        sum_mixer[:, :heads_wide],
        sum_mixer[:, heads_wide : 2 * heads_wide],
        sum_mixer[:, 2 * heads_wide : 2 * heads_wide + values_wide],
        sum_mixer[:, 2 * heads_wide + values_wide : mixer_wide],
        sum_mixer[:, mixer_wide : mixer_wide + num_heads],
        sum_mixer[:, mixer_wide + num_heads : mixer_wide + 2 * num_heads],
        sum_q_conv,
        sum_k_conv,
        sum_v_conv,
        sum_decay_log,
        sum_decay_bias,
        sum_out_gain,
        sum_inner[:, 3 * units :].T,
        sum_hidden_gain,
        sum_inner[:, :units],
        sum_inner[:, units : 2 * units],
        sum_inner[:, 2 * units : 3 * units].T,
    )


def solution(mesh):
    in_specs = (
        P(("shard", "ctx"), None),
        P("shard", None),
        P(("shard", "ctx"), None),
        P(),
        P("shard", "tp"),
        P("shard", "tp"),
        P("shard", "tp"),
        P("shard", "tp"),
        P("shard", "tp"),
        P("shard", "tp"),
        P(None, "tp"),
        P(None, "tp"),
        P(None, "tp"),
        P("tp"),
        P("tp"),
        P(),
        P("tp", "shard"),
        P(),
        P("shard", "tp"),
        P("shard", "tp"),
        P("tp", "shard"),
    )
    out_specs = (
        P(("shard", "ctx"), None),
        P(("shard", "ctx"), None),
        P(),
        P("shard", "tp"),
        P("shard", "tp"),
        P("shard", "tp"),
        P("shard", "tp"),
        P("shard", "tp"),
        P("shard", "tp"),
        P(None, "tp"),
        P(None, "tp"),
        P(None, "tp"),
        P("tp"),
        P("tp"),
        P(),
        P("tp", "shard"),
        P(),
        P("shard", "tp"),
        P("shard", "tp"),
        P("tp", "shard"),
    )
    return jax.shard_map(body, mesh=mesh, in_specs=in_specs, out_specs=out_specs, check_vma=False)
```

profile of v0, /device:TPU:0, one launch (start us, length us, event | category | flops | bytes accessed | tf_op | source)
XLA Modules:
  0.0 910.6 jit_solution(14726343507014059583)
XLA Ops:
  17.4 42.8 %all-gather.9.cloned.1.call-done = bf16[1024,1664]{1,0:T(8,128)(2,1)} async-done(((bf16[256,1664]{1,0:T(8,128)(2,1)}), bf16[1024,1664]{1,0:T(8,128)(2,1)}) %all-gather.9.cloned.1.call-update) | async-done | bytes 3407888 | tf_op jit(solution)/shard_map/all_gather | solution.py:220
  60.2 6.0 fusion.105
  101.2 3.1 fusion.37
  104.3 3.6 reshape.824
  111.7 3.2 fusion.89
  124.6 2.7 reshape.820
  141.2 3.0 copy.219
  144.2 3.1 multiply_reduce_fusion.5
  150.3 4.3 convolution_convert_fusion.4
  156.7 41.9 %reduce-scatter.7.cloned.1.call-done = bf16[256,1024]{1,0:T(8,128)(2,1)} async-done(((bf16[1024,1024]{1,0:T(8,128)(2,1)}), bf16[256,1024]{1,0:T(8,128)(2,1)}) %reduce-scatter.7.cloned.1.call-update) | async-done | bytes 524304 | tf_op jit(solution)/shard_map/reduce_scatter | solution.py:250
  204.1 37.8 %all-gather.15.cloned.1.call-done = bf16[1024,1408]{0,1:T(8,128)(2,1)} async-done(((bf16[256,1408]{0,1:T(8,128)(2,1)}), bf16[1024,1408]{0,1:T(8,128)(2,1)}) %all-gather.15.cloned.1.call-update) | async-done | bytes 2883600 | tf_op jit(solution)/shard_map/all_gather | solution.py:239
  242.0 48.0 %all-gather.13.cloned.1.call-done = bf16[1024,1024]{1,0:T(8,128)(2,1)} async-done(((bf16[256,1024]{1,0:T(8,128)(2,1)}), bf16[1024,1024]{1,0:T(8,128)(2,1)}) %all-gather.13.cloned.1.call-update) | async-done | bytes 2097168 | tf_op jit(solution)/shard_map/all_gather | solution.py:254
  290.0 8.4 fusion.265
  298.5 21.9 %all-gather.17.cloned.1.call-done = bf16[1024,704]{0,1:T(8,128)(2,1)} async-done(((bf16[256,704]{0,1:T(8,128)(2,1)}), bf16[1024,704]{0,1:T(8,128)(2,1)}) %all-gather.17.cloned.1.call-update) | async-done | bytes 1441808 | tf_op jit(solution)/shard_map/all_gather | solution.py:242
  320.3 7.7 fusion.5
  329.8 4.7 convolution_convert_fusion.3
  334.6 44.0 %reduce-scatter.11.cloned.1.call-done = bf16[256,1024]{1,0:T(8,128)(2,1)} async-done(((bf16[1024,1024]{1,0:T(8,128)(2,1)}), bf16[256,1024]{1,0:T(8,128)(2,1)}) %reduce-scatter.11.cloned.1.call-update) | async-done | bytes 524304 | tf_op jit(solution)/shard_map/reduce_scatter | solution.py:250
  382.4 2.7 fusion.246
  387.7 42.9 %all-gather.21.cloned.1.call-done = bf16[1024,1024]{1,0:T(8,128)(2,1)} async-done(((bf16[256,1024]{1,0:T(8,128)(2,1)}), bf16[1024,1024]{1,0:T(8,128)(2,1)}) %all-gather.21.cloned.1.call-update) | async-done | bytes 2097168 | tf_op jit(solution)/shard_map/all_gather | solution.py:254
  430.6 5.6 fusion.32
  442.7 2.8 fusion.266
  445.5 2.7 copy.226
  451.4 6.0 fusion.264
  457.5 2.8 fusion.18
  461.3 3.2 fusion.97
  469.5 3.5 multiply_reduce_fusion.18
  475.0 3.0 fusion.6
  512.6 3.2 convolution_add_fusion.3
  518.6 3.4 multiply_reduce_fusion.16
  553.4 5.8 concatenate.60
  559.1 8.4 convolution_convert_fusion.2
  568.9 3.1 convolution_convert_fusion.5
  573.6 7.7 convolution_convert_fusion
  581.4 4.9 fusion.39
  586.2 2.7 copy.275
  588.9 7.7 convolution_convert_fusion.1
  598.9 9.0 concatenate.61
  608.6 3.1 reduce-scatter.13.cloned.1.call-done
  613.2 43.9 %reduce-scatter.9.cloned.1.call-done = bf16[256,1024]{1,0:T(8,128)(2,1)} async-done(((bf16[1024,1024]{1,0:T(8,128)(2,1)}), bf16[256,1024]{1,0:T(8,128)(2,1)}) %reduce-scatter.9.cloned.1.call-update) | async-done | bytes 524304 | tf_op jit(solution)/shard_map/reduce_scatter | solution.py:250
  657.2 3.1 fusion.59
  660.9 44.8 %reduce-scatter.15.cloned.1.call-done = bf16[256,1664]{1,0:T(8,128)(2,1)} async-done(((bf16[1024,1664]{1,0:T(8,128)(2,1)}), bf16[256,1664]{1,0:T(8,128)(2,1)}) %reduce-scatter.15.cloned.1.call-update) | async-done | bytes 851984 | tf_op jit(solution)/shard_map/reduce_scatter | solution.py:360
  705.7 66.6 %reduce-scatter.17.cloned.1.call-done = bf16[256,2624]{1,0:T(8,128)(2,1)} async-done(((bf16[1024,2624]{1,0:T(8,128)(2,1)}), bf16[256,2624]{1,0:T(8,128)(2,1)}) %reduce-scatter.17.cloned.1.call-update) | async-done | bytes 1343504 | tf_op jit(solution)/shard_map/reduce_scatter | solution.py:360
  772.4 24.5 %all-reduce.53 = (f32[4,256]{1,0:T(4,128)}, f32[4,256]{1,0:T(4,128)}, f32[4,512]{1,0:T(4,128)}, f32[2]{0:T(128)}, f32[2]{0:T(128)}) all-reduce(f32[4,256]{1,0:T(4,128)S(1)} %pad_add_fusion.21, f32[4,256]{1,0:T(4,128)S(1)} %pad_add_fusion.20, ...), channel_id=1, replica_groups=mesh['shard'=4,'ctx'=2,'tp'=4] {'shard','ctx'}, use_global_device_ids=true, to_apply=%region_31.32 | all-reduce | flops 4100 | bytes 32800 | tf_op jit(solution)/shard_map/psum | solution.py:368
  796.9 41.0 %all-reduce.52 = (f32[1024]{0:T(1024)}, f32[256]{0:T(256)}, f32[1024]{0:T(1024)}) all-reduce(f32[1024]{0:T(1024)S(1)} %get-tuple-element.89, f32[256]{0:T(256)S(1)} %copy-done.167, f32[1024]{0:T(1024)S(1)} %copy-done.136), channel_id=1, replica_groups=mesh['shard'=4,'ctx'=2,'tp'=4] {'shard','ctx','tp'}, use_global_device_ids=true, to_apply=%region_24.25 | all-reduce | flops 2304 | bytes 18432 | tf_op jit(solution)/shard_map/psum | solution.py:365
  837.8 4.1 convert_element_type.158
  841.9 25.7 %all-gather.19.cloned.1.call-done = bf16[1024,1024]{1,0:T(8,128)(2,1)} async-done(((bf16[256,1024]{1,0:T(8,128)(2,1)}), bf16[1024,1024]{1,0:T(8,128)(2,1)}) %all-gather.19.cloned.1.call-update) | async-done | bytes 2097168 | tf_op jit(solution)/shard_map/all_gather | solution.py:254
  867.6 22.5 %all-reduce.57.cloned.1.call-done = (bf16[256,1664]{1,0:T(8,128)(2,1)}, bf16[256,2624]{1,0:T(8,128)(2,1)}) async-done(((bf16[256,1664]{1,0:T(8,128)(2,1)}, bf16[256,2624]{1,0:T(8,128)(2,1)}), (bf16[256,1664]{1,0:T(8,128)(2,1)}, bf16[256,2624]{1,0:T(8,128)(2,1)})) %all-reduce.57.cloned.1.call-update) | async-done | bytes 2195472 | tf_op jit(solution)/shard_map/psum | solution.py:361
  900.8 3.1 copy.398
  (596 shorter events, 194.2 us)
Async XLA Ops:
  7.2 53.0 %all-gather.9.cloned.1.call-start = ((), (), s32[]{:S(2)}) async-start(), calls=%async_computation.6 | async-start | bytes 4259840 | tf_op jit(solution)/shard_map/all_gather | solution.py:220
  11.2 49.0 %copy-start.134 = (f32[1024]{0:T(1024)S(1)}, f32[1024]{0:T(1024)}, u32[]{:S(2)}) copy-start(f32[1024]{0:T(1024)} %param.24) | copy-start | bytes 12292
  11.2 139.1 %all-gather.11.cloned.1.call-start = ((), (), s32[]{:S(2)}) async-start(), calls=%async_computation.7 | async-start | bytes 1310720 | tf_op jit(solution)/shard_map/all_gather | solution.py:238
  11.9 186.6 %reduce-scatter.7.cloned.1.call-start = ((), (), s32[]{:S(2)}) async-start(), calls=%async_computation.8 | async-start | bytes 2621440 | tf_op jit(solution)/shard_map/reduce_scatter | solution.py:250
  12.1 103.0 %copy-start.75 = (f32[128,128]{1,0:T(8,128)}, f32[128,128]{1,0:T(8,128)S(1)}, u32[]{:S(2)}) copy-start(f32[128,128]{1,0:T(8,128)S(1)} %fusion.183) | copy-start | bytes 196612
  12.6 53.6 %copy-start.172 = (f32[1024]{0:T(1024)}, f32[1024]{0:T(1024)S(1)}, u32[]{:S(2)}) copy-start(f32[1024]{0:T(1024)S(1)} %add_rsqrt_fusion.2) | copy-start | bytes 12292
  13.2 65.6 %copy-start.148 = (f32[1,256]{1,0:T(1,128)}, f32[1,256]{1,0:T(1,128)S(1)}, u32[]{:S(2)}) copy-start(f32[1,256]{1,0:T(1,128)S(1)} %get-tuple-element.196) | copy-start | bytes 3076
  13.2 65.6 %copy-start.150 = (f32[1,256]{1,0:T(1,128)}, f32[1,256]{1,0:T(1,128)S(1)}, u32[]{:S(2)}) copy-start(f32[1,256]{1,0:T(1,128)S(1)} %get-tuple-element.197) | copy-start | bytes 3076
  13.4 59.5 %copy-start.176 = (f32[2]{0:T(128)}, f32[2]{0:T(128)S(1)}, u32[]{:S(2)}) copy-start(f32[2]{0:T(128)S(1)} %exponential_negate_fusion) | copy-start | bytes 28
  14.0 87.1 %copy-start.126 = (f32[1,512]{1,0:T(1,128)}, f32[1,512]{1,0:T(1,128)S(1)}, u32[]{:S(2)}) copy-start(f32[1,512]{1,0:T(1,128)S(1)} %get-tuple-element.185) | copy-start | bytes 6148
  14.1 101.7 %copy-start.71 = (f32[2,128,128]{2,1,0:T(8,128)}, f32[2,128,128]{2,1,0:T(8,128)S(1)}, u32[]{:S(2)}) copy-start(f32[2,128,128]{2,1,0:T(8,128)S(1)} %broadcast_in_dim.210) | copy-start | bytes 393220
  15.6 58.8 %copy-start.162 = (pred[8,128]{1,0:T(8,128)(4,1)}, pred[8,128]{1,0:T(8,128)(4,1)S(1)}, u32[]{:S(2)}) copy-start(pred[8,128]{1,0:T(8,128)(4,1)S(1)} %get-tuple-element.131) | copy-start | bytes 3076
  15.7 85.5 %copy-start.87 = (f32[1024]{0:T(1024)}, f32[1024]{0:T(1024)S(1)}, u32[]{:S(2)}) copy-start(f32[1024]{0:T(1024)S(1)} %get-tuple-element.189) | copy-start | bytes 12292
  15.7 85.5 %copy-start.90 = (f32[1024]{0:T(1024)}, f32[1024]{0:T(1024)S(1)}, u32[]{:S(2)}) copy-start(f32[1024]{0:T(1024)S(1)} %get-tuple-element.190) | copy-start | bytes 12292
  15.7 85.5 %copy-start.93 = (f32[1024]{0:T(1024)}, f32[1024]{0:T(1024)S(1)}, u32[]{:S(2)}) copy-start(f32[1024]{0:T(1024)S(1)} %get-tuple-element.191) | copy-start | bytes 12292
  68.5 10.3 %copy-start.38 = (f32[1024,256]{1,0:T(8,128)}, f32[1024,256]{1,0:T(8,128)S(1)}, u32[]{:S(2)}) copy-start(f32[1024,256]{1,0:T(8,128)S(1)} %get-tuple-element.143) | copy-start | bytes 3145732
  71.2 7.0 collective-permute-start
  74.4 9.3 %copy-start.100 = (f32[1,2,8,128]{3,1,2,0:T(2,128)}, f32[1,2,8,128]{3,1,2,0:T(2,128)S(1)}, u32[]{:S(2)}) copy-start(f32[1,2,8,128]{3,1,2,0:T(2,128)S(1)} %fusion.357) | copy-start | bytes 24580
  75.1 8.5 copy-start.82
  76.2 31.6 %copy-start.80 = (f32[1,2,8,128]{3,2,1,0:T(8,128)}, f32[1,2,8,128]{3,2,1,0:T(8,128)S(1)}, u32[]{:S(2)}) copy-start(f32[1,2,8,128]{3,2,1,0:T(8,128)S(1)} %copy.387) | copy-start | bytes 24580
  76.2 35.4 %copy-start.98 = (f32[2,8,1,128]{3,2,1,0:T(1,128)}, f32[2,8,1,128]{3,2,1,0:T(1,128)S(1)}, u32[]{:S(2)}) copy-start(f32[2,8,1,128]{3,2,1,0:T(1,128)S(1)} %slice.340) | copy-start | bytes 24580
  85.5 12.5 %copy-start.51 = (f32[2,8,128,128]{3,2,1,0:T(8,128)}, f32[2,8,128,128]{3,2,1,0:T(8,128)S(1)}, u32[]{:S(2)}) copy-start(f32[2,8,128,128]{3,2,1,0:T(8,128)S(1)} %fusion.245) | copy-start | bytes 3145732
  120.8 23.4 %collective-permute-start.1 = (f32[2,256,128]{2,1,0:T(8,128)}, f32[2,256,128]{2,1,0:T(8,128)S(1)}, u32[]{:S(2)}, u32[]{:S(2)}) collective-permute-start(f32[2,256,128]{2,1,0:T(8,128)} %convolution_add_fusion.20), channel_id=1, source_target_pairs={{0,4},{1,5},{2,6},{3,7},{8,12},{9,13},{10,14},{11,15},{16,20},{17,... | collective-permute-start | bytes 786440 | tf_op jit(solution)/shard_map/ppermute | solution.py:14
  154.5 87.4 %all-gather.15.cloned.1.call-start = ((), (), s32[]{:S(2)}) async-start(), calls=%async_computation.10 | async-start | bytes 3604480 | tf_op jit(solution)/shard_map/all_gather | solution.py:239
  156.6 133.4 %all-gather.13.cloned.1.call-start = ((), (), s32[]{:S(2)}) async-start(), calls=%async_computation.9 | async-start | bytes 2621440 | tf_op jit(solution)/shard_map/all_gather | solution.py:254
  203.3 117.0 %all-gather.17.cloned.1.call-start = ((), (), s32[]{:S(2)}) async-start(), calls=%async_computation.11 | async-start | bytes 1802240 | tf_op jit(solution)/shard_map/all_gather | solution.py:242
  203.9 174.7 %reduce-scatter.11.cloned.1.call-start = ((), (), s32[]{:S(2)}) async-start(), calls=%async_computation.14 | async-start | bytes 2621440 | tf_op jit(solution)/shard_map/reduce_scatter | solution.py:250
  320.3 9.5 %copy-start.178 = (bf16[1024,1408]{0,1:T(8,128)(2,1)S(1)}, bf16[1024,1408]{0,1:T(8,128)(2,1)}, u32[]{:S(2)}) copy-start(bf16[1024,1408]{0,1:T(8,128)(2,1)} %all-gather.15.cloned.1.call-done) | copy-start | bytes 8650756
  334.6 96.0 %all-gather.21.cloned.1.call-start = ((), (), s32[]{:S(2)}) async-start(), calls=%async_computation.15 | async-start | bytes 2621440 | tf_op jit(solution)/shard_map/all_gather | solution.py:254
  385.1 226.5 %reduce-scatter.13.cloned.1.call-start = ((), (), s32[]{:S(2)}) async-start(), calls=%async_computation.16 | async-start | bytes 2621440 | tf_op jit(solution)/shard_map/reduce_scatter | solution.py:250
  450.1 32.5 %collective-permute-start.2 = (bf16[2,256,128]{2,1,0:T(8,128)(2,1)}, bf16[2,256,128]{2,1,0:T(8,128)(2,1)}, u32[]{:S(2)}, u32[]{:S(2)}) collective-permute-start(bf16[2,256,128]{2,1,0:T(8,128)(2,1)} %fusion.44), channel_id=1, source_target_pairs={{4,0},{5,1},{6,2},{7,3},{12,8},{13,9},{14,10},{15,11},{20,16},{21,... | collective-permute-start | bytes 393224 | tf_op jit(solution)/shard_map/ppermute | solution.py:14
  512.6 11.2 %slice-start = ((s8[6815744]{0:T(1024)(128)(4,1)}), s8[4194304]{0:T(1024)(128)(4,1)S(1)}, s32[]{:S(2)}) async-start(s8[6815744]{0:T(1024)(128)(4,1)} %bitcast.463), calls=%async_computation.21 | async-start | bytes 8388608
  546.6 3.8 collective-permute-start.3
  559.1 8.5 copy-start.184
  567.6 89.6 %reduce-scatter.9.cloned.1.call-start = ((), (), s32[]{:S(2)}) async-start(), calls=%async_computation.12 | async-start | bytes 2621440 | tf_op jit(solution)/shard_map/reduce_scatter | solution.py:250
  572.1 133.7 %reduce-scatter.15.cloned.1.call-start = ((), (), s32[]{:S(2)}) async-start(), calls=%async_computation.18 | async-start | bytes 4259840 | tf_op jit(solution)/shard_map/reduce_scatter | solution.py:360
  581.3 191.0 %reduce-scatter.17.cloned.1.call-start = ((), (), s32[]{:S(2)}) async-start(), calls=%async_computation.19 | async-start | bytes 6881280 | tf_op jit(solution)/shard_map/reduce_scatter | solution.py:360
  607.9 49.2 %copy-start.24 = (bf16[256,1024]{1,0:T(8,128)(2,1)S(1)}, bf16[256,1024]{1,0:T(8,128)(2,1)}, u32[]{:S(2)}) copy-start(bf16[256,1024]{1,0:T(8,128)(2,1)} %reduce-scatter.7.cloned.1.call-done) | copy-start | bytes 1572868
  607.9 49.2 %copy-start.49 = (bf16[256,1024]{1,0:T(8,128)(2,1)S(1)}, bf16[256,1024]{1,0:T(8,128)(2,1)}, u32[]{:S(2)}) copy-start(bf16[256,1024]{1,0:T(8,128)(2,1)} %reduce-scatter.11.cloned.1.call-done) | copy-start | bytes 1572868
  607.9 49.2 %copy-start.115 = (f32[1024]{0:T(1024)S(1)}, f32[1024]{0:T(1024)}, u32[]{:S(2)}) copy-start(f32[1024]{0:T(1024)} %param.38) | copy-start | bytes 12292
  608.0 49.2 %copy-start.123 = (f32[256]{0:T(256)S(1)}, f32[256]{0:T(256)}, u32[]{:S(2)}) copy-start(f32[256]{0:T(256)} %copy-done.122) | copy-start | bytes 3076
  608.0 49.2 %copy-start.147 = (f32[256]{0:T(256)S(1)}, f32[256]{0:T(256)}, u32[]{:S(2)}) copy-start(f32[256]{0:T(256)} %copy-done.146) | copy-start | bytes 3076
  608.0 229.8 %all-gather.23.cloned.1.call-start = ((), (), s32[]{:S(2)}) async-start(), calls=%async_computation.17 | async-start | bytes 2621440 | tf_op jit(solution)/shard_map/all_gather | solution.py:254
  660.3 112.1 %copy-start.181 = (f32[2]{0:T(128)S(1)}, f32[2]{0:T(128)}, u32[]{:S(2)}) copy-start(f32[2]{0:T(128)} %param.34) | copy-start | bytes 28
  660.3 136.6 %copy-start.136 = (f32[1024]{0:T(1024)S(1)}, f32[1024]{0:T(1024)}, u32[]{:S(2)}) copy-start(f32[1024]{0:T(1024)} %get-tuple-element.87) | copy-start | bytes 12292
  660.3 136.6 %copy-start.167 = (f32[256]{0:T(256)S(1)}, f32[256]{0:T(256)}, u32[]{:S(2)}) copy-start(f32[256]{0:T(256)} %get-tuple-element.82) | copy-start | bytes 3076
  660.3 207.3 %all-gather.19.cloned.1.call-start = ((), (), s32[]{:S(2)}) async-start(), calls=%async_computation.13 | async-start | bytes 2621440 | tf_op jit(solution)/shard_map/all_gather | solution.py:254
  660.9 229.2 %all-reduce.57.cloned.1.call-start = ((), (), s32[]{:S(2)}) async-start(), calls=%async_computation.20 | async-start | bytes 4456448 | tf_op jit(solution)/shard_map/psum | solution.py:361
  (158 other events, 385.1 us)
Sparse Core Ops, SparseCore 0:
  11.3 48.8 all-gather.8
  62.0 26.4 all-gather.10
  154.7 43.8 reduce-scatter.6
  201.0 40.9 all-gather.14
  244.0 45.9 all-gather.12
  291.8 28.4 all-gather.16
  334.7 43.8 reduce-scatter.10
  385.3 45.2 all-gather.20
  567.7 43.9 reduce-scatter.12
  613.9 43.1 reduce-scatter.8
  660.2 45.4 reduce-scatter.14
  708.6 63.6 reduce-scatter.16
  774.4 46.3 all-gather.22
  822.8 44.7 all-gather.18
  869.9 20.1 all-reduce.56
where the time goes:
time: 920 us; the launch traced here: 911 us
  waiting for transfers between devices  488 us (53%)
  matrix products  160 us (17%)
  local copies, waits for them, and re-layouts  101 us (11%)
  other arithmetic  72.8 us (8%)
  blocking collectives  65.5 us (7%)
  between operations  16.8 us (2%)
    reduce_scatter x4, waiting for transfers between devices, sum_rows(): lax.psum_scatter(array.astype(low), 'tp', scatter_dimension=0, tiled=True)  133 us
    all_gather x4, waiting for transfers between devices, all_rows(): return lax.all_gather(array, 'tp', axis=0, tiled=True)  117 us
    reduce_scatter x2, waiting for transfers between devices, sum_weight(): lax.psum_scatter(array.astype(low), 'shard', scatter_dimension=0, tiled=T...  111 us
    dot_general x59, matrix products, dot_high(): return jnp.einsum(equation, left, right, precision=PRECISE)  86.5 us
    all_gather x1, waiting for transfers between devices, body(): lax.all_gather(jnp.concatenate([query_weight, key_weight, value_weight, g...  42.8 us
    psum x1, blocking collectives, body(): lax.psum((grad_mixer_gain, grad_hidden_gain, grad_out_gain), ('shard', 'c...  41 us
    all_gather x1, waiting for transfers between devices, body(): lax.all_gather(jnp.concatenate([hidden_gate, hidden_up], axis=1), 'shard'...  37.8 us
    unnamed x387, local copies, waits for them, and re-layouts  35.2 us
  transfers between devices with their start and end apart: 19, of which 13 were waited for; matrix products, arithmetic and copies ran while one was open for 20% of the time, Pallas kernels for 0%

commit v1 on v0

--- a/solution.py
+++ b/solution.py
@@ -366,7 +366,8 @@
         (grad_mixer_gain, grad_hidden_gain, grad_out_gain), ("shard", "ctx", "tp")
     )
     sum_q_conv, sum_k_conv, sum_v_conv, sum_decay_log, sum_decay_bias = lax.psum(
-        (grad_q_conv, grad_k_conv, grad_v_conv, grad_decay_log, grad_decay_bias), ("shard", "ctx")
+        lax.psum((grad_q_conv, grad_k_conv, grad_v_conv, grad_decay_log, grad_decay_bias), "ctx"),
+        "shard",
     )
     return (
         block_out,

time: 920 us -> 920 us (level)
    psum x1, blocking collectives: 24.5 us -> 3.41 us  [body(): lax.psum((grad_q_conv, grad_k_conv, grad_v_conv, grad_decay_log, grad_dec...]
    psum x0 -> x1, blocking collectives: none -> 15.8 us  [body(): lax.psum(lax.psum((grad_q_conv, grad_k_conv, grad_v_conv, grad_decay_log,...]
where the time goes in v1:
time: 920 us; the launch traced here: 911 us
  waiting for transfers between devices  494 us (54%)
  matrix products  160 us (17%)
  local copies, waits for them, and re-layouts  101 us (11%)
  other arithmetic  72.8 us (8%)
  blocking collectives  60 us (7%)
  between operations  16.8 us (2%)
    reduce_scatter x4, waiting for transfers between devices, sum_rows(): lax.psum_scatter(array.astype(low), 'tp', scatter_dimension=0, tiled=True)  133 us
    all_gather x4, waiting for transfers between devices, all_rows(): return lax.all_gather(array, 'tp', axis=0, tiled=True)  122 us
    reduce_scatter x2, waiting for transfers between devices, sum_weight(): lax.psum_scatter(array.astype(low), 'shard', scatter_dimension=0, tiled=T...  111 us
    dot_general x59, matrix products, dot_high(): return jnp.einsum(equation, left, right, precision=PRECISE)  86.5 us
    all_gather x1, waiting for transfers between devices, body(): lax.all_gather(jnp.concatenate([query_weight, key_weight, value_weight, g...  42.8 us
    psum x1, blocking collectives, body(): lax.psum((grad_mixer_gain, grad_hidden_gain, grad_out_gain), ('shard', 'c...  40.8 us
    all_gather x1, waiting for transfers between devices, body(): lax.all_gather(jnp.concatenate([hidden_gate, hidden_up], axis=1), 'shard'...  37.8 us
    unnamed x387, local copies, waits for them, and re-layouts  35.3 us
  transfers between devices with their start and end apart: 19, of which 13 were waited for; matrix products, arithmetic and copies ran while one was open for 20% of the time, Pallas kernels for 0%

profile of v1, /device:TPU:0, one launch (start us, length us, event | category | flops | bytes accessed | tf_op | source)
XLA Modules:
  0.0 910.9 jit_solution(17294539100570969836)
XLA Ops:
  17.4 42.8 %all-gather.9.cloned.1.call-done = bf16[1024,1664]{1,0:T(8,128)(2,1)} async-done(((bf16[256,1664]{1,0:T(8,128)(2,1)}), bf16[1024,1664]{1,0:T(8,128)(2,1)}) %all-gather.9.cloned.1.call-update) | async-done | bytes 3407888 | tf_op jit(solution)/shard_map/all_gather | solution.py:220
  60.2 6.0 fusion.105
  101.2 3.1 fusion.37
  104.3 3.5 reshape.824
  111.7 3.2 fusion.89
  124.6 2.7 reshape.820
  141.1 3.0 copy.219
  144.1 3.1 multiply_reduce_fusion.5
  150.2 4.3 convolution_convert_fusion.4
  156.7 41.9 %reduce-scatter.7.cloned.1.call-done = bf16[256,1024]{1,0:T(8,128)(2,1)} async-done(((bf16[1024,1024]{1,0:T(8,128)(2,1)}), bf16[256,1024]{1,0:T(8,128)(2,1)}) %reduce-scatter.7.cloned.1.call-update) | async-done | bytes 524304 | tf_op jit(solution)/shard_map/reduce_scatter | solution.py:250
  204.2 37.8 %all-gather.15.cloned.1.call-done = bf16[1024,1408]{0,1:T(8,128)(2,1)} async-done(((bf16[256,1408]{0,1:T(8,128)(2,1)}), bf16[1024,1408]{0,1:T(8,128)(2,1)}) %all-gather.15.cloned.1.call-update) | async-done | bytes 2883600 | tf_op jit(solution)/shard_map/all_gather | solution.py:239
  242.0 48.0 %all-gather.13.cloned.1.call-done = bf16[1024,1024]{1,0:T(8,128)(2,1)} async-done(((bf16[256,1024]{1,0:T(8,128)(2,1)}), bf16[1024,1024]{1,0:T(8,128)(2,1)}) %all-gather.13.cloned.1.call-update) | async-done | bytes 2097168 | tf_op jit(solution)/shard_map/all_gather | solution.py:254
  290.0 8.4 fusion.265
  298.5 21.9 %all-gather.17.cloned.1.call-done = bf16[1024,704]{0,1:T(8,128)(2,1)} async-done(((bf16[256,704]{0,1:T(8,128)(2,1)}), bf16[1024,704]{0,1:T(8,128)(2,1)}) %all-gather.17.cloned.1.call-update) | async-done | bytes 1441808 | tf_op jit(solution)/shard_map/all_gather | solution.py:242
  320.3 7.7 fusion.5
  329.8 4.7 convolution_convert_fusion.3
  334.7 44.0 %reduce-scatter.11.cloned.1.call-done = bf16[256,1024]{1,0:T(8,128)(2,1)} async-done(((bf16[1024,1024]{1,0:T(8,128)(2,1)}), bf16[256,1024]{1,0:T(8,128)(2,1)}) %reduce-scatter.11.cloned.1.call-update) | async-done | bytes 524304 | tf_op jit(solution)/shard_map/reduce_scatter | solution.py:250
  382.4 2.7 fusion.246
  387.7 42.9 %all-gather.21.cloned.1.call-done = bf16[1024,1024]{1,0:T(8,128)(2,1)} async-done(((bf16[256,1024]{1,0:T(8,128)(2,1)}), bf16[1024,1024]{1,0:T(8,128)(2,1)}) %all-gather.21.cloned.1.call-update) | async-done | bytes 2097168 | tf_op jit(solution)/shard_map/all_gather | solution.py:254
  430.6 5.6 fusion.32
  442.7 2.8 fusion.266
  445.5 2.7 copy.226
  451.5 6.0 fusion.264
  457.5 2.8 fusion.18
  461.3 3.2 fusion.97
  469.5 3.5 multiply_reduce_fusion.18
  475.0 3.0 fusion.6
  512.6 3.2 convolution_add_fusion.3
  518.5 3.4 multiply_reduce_fusion.16
  553.3 5.8 concatenate.60
  559.1 8.4 convolution_convert_fusion.2
  568.9 3.1 convolution_convert_fusion.5
  573.6 7.7 convolution_convert_fusion
  581.3 4.9 fusion.39
  588.9 7.7 convolution_convert_fusion.1
  598.9 9.0 concatenate.61
  608.5 3.1 reduce-scatter.13.cloned.1.call-done
  613.2 43.9 %reduce-scatter.9.cloned.1.call-done = bf16[256,1024]{1,0:T(8,128)(2,1)} async-done(((bf16[1024,1024]{1,0:T(8,128)(2,1)}), bf16[256,1024]{1,0:T(8,128)(2,1)}) %reduce-scatter.9.cloned.1.call-update) | async-done | bytes 524304 | tf_op jit(solution)/shard_map/reduce_scatter | solution.py:250
  657.1 3.1 fusion.59
  660.9 44.8 %reduce-scatter.15.cloned.1.call-done = bf16[256,1664]{1,0:T(8,128)(2,1)} async-done(((bf16[1024,1664]{1,0:T(8,128)(2,1)}), bf16[256,1664]{1,0:T(8,128)(2,1)}) %reduce-scatter.15.cloned.1.call-update) | async-done | bytes 851984 | tf_op jit(solution)/shard_map/reduce_scatter | solution.py:360
  705.7 66.6 %reduce-scatter.17.cloned.1.call-done = bf16[256,2624]{1,0:T(8,128)(2,1)} async-done(((bf16[1024,2624]{1,0:T(8,128)(2,1)}), bf16[256,2624]{1,0:T(8,128)(2,1)}) %reduce-scatter.17.cloned.1.call-update) | async-done | bytes 1343504 | tf_op jit(solution)/shard_map/reduce_scatter | solution.py:360
  772.3 3.4 all-reduce.54
  775.7 15.8 %all-reduce.53 = (f32[4,256]{1,0:T(4,128)}, f32[4,256]{1,0:T(4,128)}, f32[4,512]{1,0:T(4,128)}, f32[2]{0:T(128)}, f32[2]{0:T(128)}) all-reduce(f32[4,256]{1,0:T(4,128)S(1)} %get-tuple-element.120, f32[4,256]{1,0:T(4,128)S(1)} %get-tuple-element.121, ...), channel_id=1, replica_groups=mesh['shard'=4,'ctx'=2,'tp'=4] {'shard'}, use_global_device_ids=true, to_apply=%region_32.33 | all-reduce | flops 4100 | bytes 32800 | tf_op jit(solution)/shard_map/psum | solution.py:368
  791.6 40.8 %all-reduce.52 = (f32[1024]{0:T(1024)}, f32[256]{0:T(256)}, f32[1024]{0:T(1024)}) all-reduce(f32[1024]{0:T(1024)S(1)} %get-tuple-element.89, f32[256]{0:T(256)S(1)} %copy-done.167, f32[1024]{0:T(1024)S(1)} %copy-done.136), channel_id=1, replica_groups=mesh['shard'=4,'ctx'=2,'tp'=4] {'shard','ctx','tp'}, use_global_device_ids=true, to_apply=%region_24.25 | all-reduce | flops 2304 | bytes 18432 | tf_op jit(solution)/shard_map/psum | solution.py:365
  832.4 4.1 convert_element_type.158
  836.4 31.5 %all-gather.19.cloned.1.call-done = bf16[1024,1024]{1,0:T(8,128)(2,1)} async-done(((bf16[256,1024]{1,0:T(8,128)(2,1)}), bf16[1024,1024]{1,0:T(8,128)(2,1)}) %all-gather.19.cloned.1.call-update) | async-done | bytes 2097168 | tf_op jit(solution)/shard_map/all_gather | solution.py:254
  868.0 22.4 %all-reduce.58.cloned.1.call-done = (bf16[256,1664]{1,0:T(8,128)(2,1)}, bf16[256,2624]{1,0:T(8,128)(2,1)}) async-done(((bf16[256,1664]{1,0:T(8,128)(2,1)}, bf16[256,2624]{1,0:T(8,128)(2,1)}), (bf16[256,1664]{1,0:T(8,128)(2,1)}, bf16[256,2624]{1,0:T(8,128)(2,1)})) %all-reduce.58.cloned.1.call-update) | async-done | bytes 2195472 | tf_op jit(solution)/shard_map/psum | solution.py:361
  901.1 3.1 copy.398
  (597 shorter events, 196.9 us)
Async XLA Ops:
  7.2 53.0 %all-gather.9.cloned.1.call-start = ((), (), s32[]{:S(2)}) async-start(), calls=%async_computation.6 | async-start | bytes 4259840 | tf_op jit(solution)/shard_map/all_gather | solution.py:220
  11.2 49.0 %copy-start.134 = (f32[1024]{0:T(1024)S(1)}, f32[1024]{0:T(1024)}, u32[]{:S(2)}) copy-start(f32[1024]{0:T(1024)} %param.24) | copy-start | bytes 12292
  11.2 139.1 %all-gather.11.cloned.1.call-start = ((), (), s32[]{:S(2)}) async-start(), calls=%async_computation.7 | async-start | bytes 1310720 | tf_op jit(solution)/shard_map/all_gather | solution.py:238
  11.9 186.6 %reduce-scatter.7.cloned.1.call-start = ((), (), s32[]{:S(2)}) async-start(), calls=%async_computation.8 | async-start | bytes 2621440 | tf_op jit(solution)/shard_map/reduce_scatter | solution.py:250
  12.1 103.0 %copy-start.75 = (f32[128,128]{1,0:T(8,128)}, f32[128,128]{1,0:T(8,128)S(1)}, u32[]{:S(2)}) copy-start(f32[128,128]{1,0:T(8,128)S(1)} %fusion.183) | copy-start | bytes 196612
  12.6 53.6 %copy-start.172 = (f32[1024]{0:T(1024)}, f32[1024]{0:T(1024)S(1)}, u32[]{:S(2)}) copy-start(f32[1024]{0:T(1024)S(1)} %add_rsqrt_fusion.2) | copy-start | bytes 12292
  13.2 65.6 %copy-start.148 = (f32[1,256]{1,0:T(1,128)}, f32[1,256]{1,0:T(1,128)S(1)}, u32[]{:S(2)}) copy-start(f32[1,256]{1,0:T(1,128)S(1)} %get-tuple-element.201) | copy-start | bytes 3076
  13.2 65.6 %copy-start.150 = (f32[1,256]{1,0:T(1,128)}, f32[1,256]{1,0:T(1,128)S(1)}, u32[]{:S(2)}) copy-start(f32[1,256]{1,0:T(1,128)S(1)} %get-tuple-element.202) | copy-start | bytes 3076
  13.4 59.5 %copy-start.176 = (f32[2]{0:T(128)}, f32[2]{0:T(128)S(1)}, u32[]{:S(2)}) copy-start(f32[2]{0:T(128)S(1)} %exponential_negate_fusion) | copy-start | bytes 28
  14.0 87.1 %copy-start.126 = (f32[1,512]{1,0:T(1,128)}, f32[1,512]{1,0:T(1,128)S(1)}, u32[]{:S(2)}) copy-start(f32[1,512]{1,0:T(1,128)S(1)} %get-tuple-element.190) | copy-start | bytes 6148
  14.0 101.7 %copy-start.71 = (f32[2,128,128]{2,1,0:T(8,128)}, f32[2,128,128]{2,1,0:T(8,128)S(1)}, u32[]{:S(2)}) copy-start(f32[2,128,128]{2,1,0:T(8,128)S(1)} %broadcast_in_dim.210) | copy-start | bytes 393220
  15.5 58.9 %copy-start.162 = (pred[8,128]{1,0:T(8,128)(4,1)}, pred[8,128]{1,0:T(8,128)(4,1)S(1)}, u32[]{:S(2)}) copy-start(pred[8,128]{1,0:T(8,128)(4,1)S(1)} %get-tuple-element.136) | copy-start | bytes 3076
  15.6 85.5 %copy-start.87 = (f32[1024]{0:T(1024)}, f32[1024]{0:T(1024)S(1)}, u32[]{:S(2)}) copy-start(f32[1024]{0:T(1024)S(1)} %get-tuple-element.194) | copy-start | bytes 12292
  15.6 85.5 %copy-start.90 = (f32[1024]{0:T(1024)}, f32[1024]{0:T(1024)S(1)}, u32[]{:S(2)}) copy-start(f32[1024]{0:T(1024)S(1)} %get-tuple-element.195) | copy-start | bytes 12292
  15.6 85.5 %copy-start.93 = (f32[1024]{0:T(1024)}, f32[1024]{0:T(1024)S(1)}, u32[]{:S(2)}) copy-start(f32[1024]{0:T(1024)S(1)} %get-tuple-element.196) | copy-start | bytes 12292
  68.5 10.3 %copy-start.38 = (f32[1024,256]{1,0:T(8,128)}, f32[1024,256]{1,0:T(8,128)S(1)}, u32[]{:S(2)}) copy-start(f32[1024,256]{1,0:T(8,128)S(1)} %get-tuple-element.148) | copy-start | bytes 3145732
  71.2 7.0 collective-permute-start
  74.4 9.2 %copy-start.100 = (f32[1,2,8,128]{3,1,2,0:T(2,128)}, f32[1,2,8,128]{3,1,2,0:T(2,128)S(1)}, u32[]{:S(2)}) copy-start(f32[1,2,8,128]{3,1,2,0:T(2,128)S(1)} %fusion.357) | copy-start | bytes 24580
  75.2 8.5 copy-start.82
  76.2 31.6 %copy-start.80 = (f32[1,2,8,128]{3,2,1,0:T(8,128)}, f32[1,2,8,128]{3,2,1,0:T(8,128)S(1)}, u32[]{:S(2)}) copy-start(f32[1,2,8,128]{3,2,1,0:T(8,128)S(1)} %copy.387) | copy-start | bytes 24580
  76.3 35.4 %copy-start.98 = (f32[2,8,1,128]{3,2,1,0:T(1,128)}, f32[2,8,1,128]{3,2,1,0:T(1,128)S(1)}, u32[]{:S(2)}) copy-start(f32[2,8,1,128]{3,2,1,0:T(1,128)S(1)} %slice.340) | copy-start | bytes 24580
  85.5 12.5 %copy-start.51 = (f32[2,8,128,128]{3,2,1,0:T(8,128)}, f32[2,8,128,128]{3,2,1,0:T(8,128)S(1)}, u32[]{:S(2)}) copy-start(f32[2,8,128,128]{3,2,1,0:T(8,128)S(1)} %fusion.245) | copy-start | bytes 3145732
  120.8 23.4 %collective-permute-start.1 = (f32[2,256,128]{2,1,0:T(8,128)}, f32[2,256,128]{2,1,0:T(8,128)S(1)}, u32[]{:S(2)}, u32[]{:S(2)}) collective-permute-start(f32[2,256,128]{2,1,0:T(8,128)} %convolution_add_fusion.20), channel_id=1, source_target_pairs={{0,4},{1,5},{2,6},{3,7},{8,12},{9,13},{10,14},{11,15},{16,20},{17,... | collective-permute-start | bytes 786440 | tf_op jit(solution)/shard_map/ppermute | solution.py:14
  154.5 87.4 %all-gather.15.cloned.1.call-start = ((), (), s32[]{:S(2)}) async-start(), calls=%async_computation.10 | async-start | bytes 3604480 | tf_op jit(solution)/shard_map/all_gather | solution.py:239
  156.6 133.4 %all-gather.13.cloned.1.call-start = ((), (), s32[]{:S(2)}) async-start(), calls=%async_computation.9 | async-start | bytes 2621440 | tf_op jit(solution)/shard_map/all_gather | solution.py:254
  203.4 116.9 %all-gather.17.cloned.1.call-start = ((), (), s32[]{:S(2)}) async-start(), calls=%async_computation.11 | async-start | bytes 1802240 | tf_op jit(solution)/shard_map/all_gather | solution.py:242
  204.0 174.6 %reduce-scatter.11.cloned.1.call-start = ((), (), s32[]{:S(2)}) async-start(), calls=%async_computation.14 | async-start | bytes 2621440 | tf_op jit(solution)/shard_map/reduce_scatter | solution.py:250
  320.3 9.5 %copy-start.178 = (bf16[1024,1408]{0,1:T(8,128)(2,1)S(1)}, bf16[1024,1408]{0,1:T(8,128)(2,1)}, u32[]{:S(2)}) copy-start(bf16[1024,1408]{0,1:T(8,128)(2,1)} %all-gather.15.cloned.1.call-done) | copy-start | bytes 8650756
  334.6 96.0 %all-gather.21.cloned.1.call-start = ((), (), s32[]{:S(2)}) async-start(), calls=%async_computation.15 | async-start | bytes 2621440 | tf_op jit(solution)/shard_map/all_gather | solution.py:254
  385.2 226.4 %reduce-scatter.13.cloned.1.call-start = ((), (), s32[]{:S(2)}) async-start(), calls=%async_computation.16 | async-start | bytes 2621440 | tf_op jit(solution)/shard_map/reduce_scatter | solution.py:250
  450.1 32.4 %collective-permute-start.2 = (bf16[2,256,128]{2,1,0:T(8,128)(2,1)}, bf16[2,256,128]{2,1,0:T(8,128)(2,1)}, u32[]{:S(2)}, u32[]{:S(2)}) collective-permute-start(bf16[2,256,128]{2,1,0:T(8,128)(2,1)} %fusion.44), channel_id=1, source_target_pairs={{4,0},{5,1},{6,2},{7,3},{12,8},{13,9},{14,10},{15,11},{20,16},{21,... | collective-permute-start | bytes 393224 | tf_op jit(solution)/shard_map/ppermute | solution.py:14
  512.6 11.2 %slice-start = ((s8[6815744]{0:T(1024)(128)(4,1)}), s8[4194304]{0:T(1024)(128)(4,1)S(1)}, s32[]{:S(2)}) async-start(s8[6815744]{0:T(1024)(128)(4,1)} %bitcast.463), calls=%async_computation.21 | async-start | bytes 8388608
  546.6 3.8 collective-permute-start.3
  559.1 8.5 copy-start.184
  567.5 89.6 %reduce-scatter.9.cloned.1.call-start = ((), (), s32[]{:S(2)}) async-start(), calls=%async_computation.12 | async-start | bytes 2621440 | tf_op jit(solution)/shard_map/reduce_scatter | solution.py:250
  572.0 133.7 %reduce-scatter.15.cloned.1.call-start = ((), (), s32[]{:S(2)}) async-start(), calls=%async_computation.18 | async-start | bytes 4259840 | tf_op jit(solution)/shard_map/reduce_scatter | solution.py:360
  581.2 191.0 %reduce-scatter.17.cloned.1.call-start = ((), (), s32[]{:S(2)}) async-start(), calls=%async_computation.19 | async-start | bytes 6881280 | tf_op jit(solution)/shard_map/reduce_scatter | solution.py:360
  607.9 49.3 %copy-start.24 = (bf16[256,1024]{1,0:T(8,128)(2,1)S(1)}, bf16[256,1024]{1,0:T(8,128)(2,1)}, u32[]{:S(2)}) copy-start(bf16[256,1024]{1,0:T(8,128)(2,1)} %reduce-scatter.7.cloned.1.call-done) | copy-start | bytes 1572868
  607.9 49.3 %copy-start.49 = (bf16[256,1024]{1,0:T(8,128)(2,1)S(1)}, bf16[256,1024]{1,0:T(8,128)(2,1)}, u32[]{:S(2)}) copy-start(bf16[256,1024]{1,0:T(8,128)(2,1)} %reduce-scatter.11.cloned.1.call-done) | copy-start | bytes 1572868
  607.9 49.2 %copy-start.115 = (f32[1024]{0:T(1024)S(1)}, f32[1024]{0:T(1024)}, u32[]{:S(2)}) copy-start(f32[1024]{0:T(1024)} %param.38) | copy-start | bytes 12292
  607.9 49.2 %copy-start.123 = (f32[256]{0:T(256)S(1)}, f32[256]{0:T(256)}, u32[]{:S(2)}) copy-start(f32[256]{0:T(256)} %copy-done.122) | copy-start | bytes 3076
  607.9 49.2 %copy-start.147 = (f32[256]{0:T(256)S(1)}, f32[256]{0:T(256)}, u32[]{:S(2)}) copy-start(f32[256]{0:T(256)} %copy-done.146) | copy-start | bytes 3076
  607.9 224.4 %all-gather.23.cloned.1.call-start = ((), (), s32[]{:S(2)}) async-start(), calls=%async_computation.17 | async-start | bytes 2621440 | tf_op jit(solution)/shard_map/all_gather | solution.py:254
  660.2 112.1 %copy-start.181 = (f32[2]{0:T(128)S(1)}, f32[2]{0:T(128)}, u32[]{:S(2)}) copy-start(f32[2]{0:T(128)} %param.34) | copy-start | bytes 28
  660.2 131.3 %copy-start.136 = (f32[1024]{0:T(1024)S(1)}, f32[1024]{0:T(1024)}, u32[]{:S(2)}) copy-start(f32[1024]{0:T(1024)} %get-tuple-element.87) | copy-start | bytes 12292
  660.2 131.3 %copy-start.167 = (f32[256]{0:T(256)S(1)}, f32[256]{0:T(256)}, u32[]{:S(2)}) copy-start(f32[256]{0:T(256)} %get-tuple-element.82) | copy-start | bytes 3076
  660.3 207.7 %all-gather.19.cloned.1.call-start = ((), (), s32[]{:S(2)}) async-start(), calls=%async_computation.13 | async-start | bytes 2621440 | tf_op jit(solution)/shard_map/all_gather | solution.py:254
  660.8 229.5 %all-reduce.58.cloned.1.call-start = ((), (), s32[]{:S(2)}) async-start(), calls=%async_computation.20 | async-start | bytes 4456448 | tf_op jit(solution)/shard_map/psum | solution.py:361
  (158 other events, 385.1 us)
Sparse Core Ops, SparseCore 0:
  11.3 48.8 all-gather.8
  62.0 26.4 all-gather.10
  154.6 43.8 reduce-scatter.6
  201.0 40.9 all-gather.14
  244.0 45.9 all-gather.12
  291.8 28.4 all-gather.16
  334.7 43.8 reduce-scatter.10
  385.3 45.2 all-gather.20
  567.6 43.9 reduce-scatter.12
  613.9 43.1 reduce-scatter.8
  660.2 45.4 reduce-scatter.14
  708.6 63.6 reduce-scatter.16
  774.4 46.7 all-gather.22
  823.2 44.7 all-gather.18
  870.2 20.1 all-reduce.57
